TPU v7x, 32 devices: a whole 2x2x4 slice. The times are simulated.
32 devices in a mesh: section: 2 (over y), expert: 4 (over z), dp: 4 (over x, core).
Axes of the slice: x: 2, y: 2, z: 4, core: 2. Of those that a mesh axis runs over, the one named last changes fastest.
Arguments:
- residual: bfloat16 [4096, 2048], P(('section', 'expert', 'dp')), may hold values from -12 to 12
- queries: bfloat16 [4096, 1024], P(('section', 'expert', 'dp')), may hold values from -6 to 6
- attn_keys: bfloat16 [4096, 1024], P(('section', 'expert', 'dp')), may hold values from -6 to 6
- attn_values: bfloat16 [4096, 1024], P(('section', 'expert', 'dp')), may hold values from -6 to 6
- out_weight: bfloat16 [1024, 2048], P('expert'), may hold values from -0.1875 to 0.1875
- norm_gain: float32 [2048], replicated, may hold values from 0.25 to 1.75
- gate_weight: bfloat16 [4, 2048, 4096], P('expert', None, 'dp'), may hold values from -0.125 to 0.125
- up_weight: bfloat16 [4, 2048, 4096], P('expert', None, 'dp'), may hold values from -0.125 to 0.125
- down_weight: bfloat16 [4, 4096, 2048], P('expert', 'dp'), may hold values from -0.09375 to 0.09375
- expert_ids: int32 [4096, 1], P(('section', 'expert', 'dp')), may hold values from 0 to 3; in each aligned block of 128 rows (0 to 127, 128 to 255, ...) at most 64 rows name the same one
- out_grad: bfloat16 [4096, 2048], P(('section', 'expert', 'dp')), may hold values from -6 to 6
Outputs:
- layer_out: bfloat16 [4096, 2048], P(('section', 'expert', 'dp'))
- resid_grad: bfloat16 [4096, 2048], P(('section', 'expert', 'dp'))
- query_grad: bfloat16 [4096, 1024], P(('section', 'expert', 'dp'))
- key_grad: bfloat16 [4096, 1024], P(('section', 'expert', 'dp'))
- value_grad: bfloat16 [4096, 1024], P(('section', 'expert', 'dp'))
- weight_grad: float32 [1024, 2048], P('expert')
Inputs may be any that keep to these rules, and one draw needn't show every extreme that they name: `expert_ids`: no expert is named by more than 64 of the 128 rows of one device (an aligned block); in every draw some block names one expert exactly 64 times.
All inputs are finite; a program needn't handle non-finite values.
Results may differ from a plain program's by a relative error of at most 0.023.
Values may be sent and summed in bfloat16 or wider, within the bound.
A program may use at most 128 MiB of HBM per device.

v0:
```python
import math
import jax
import jax.numpy as jnp
from jax import lax
from jax.sharding import PartitionSpec as P

D = 2048
HEADS = 8
HEAD = 128
A = 1024
FF = 4096
epsilon = 1e-06


def contract_last(left_side, right_side):
    return lax.dot_general(
        left_side, right_side, (((1,), (1,)), ((), ())), preferred_element_type=jnp.float32
    )


def contract_first(left_side, right_side):
    return lax.dot_general(
        left_side, right_side, (((0,), (0,)), ((), ())), preferred_element_type=jnp.float32
    )


def shards(
    residual,
    queries,
    attn_keys,
    attn_values,
    out_weight,
    norm_gain,
    gate_weight,
    up_weight,
    down_weight,
    expert_ids,
    out_grad,
):
    tokens_here = residual.shape[0]
    experts = lax.axis_size("expert")
    data_ways = lax.axis_size("dp")
    capacity = max(tokens_here // 8, 2 * tokens_here // experts)
    inv_root = 1.0 / math.sqrt(HEAD)
    keys_all, values_all = (
        lax.all_gather(attn_keys, "dp", axis=0, tiled=True),
        lax.all_gather(attn_values, "dp", axis=0, tiled=True),
    )
    query_heads = queries.reshape(tokens_here, HEADS, HEAD)
    key_heads = keys_all.reshape(-1, HEADS, HEAD)
    value_heads = values_all.reshape(-1, HEADS, HEAD)
    scores = (
        jnp.einsum("thd,shd->hts", query_heads, key_heads, preferred_element_type=jnp.float32)
        * inv_root
    )
    row_peak = jnp.max(scores, axis=-1, keepdims=True)
    exp_scores = jnp.exp(scores - row_peak)
    attn_probs = exp_scores / jnp.sum(exp_scores, axis=-1, keepdims=True)
    probs_low = attn_probs.astype(jnp.bfloat16)
    attended = (
        jnp.einsum("hts,shd->thd", probs_low, value_heads, preferred_element_type=jnp.float32)
        .reshape(tokens_here, A)
        .astype(jnp.bfloat16)
    )
    full_out = lax.all_gather(out_weight, "expert", axis=0, tiled=True)
    hidden = residual.astype(jnp.float32) + jnp.dot(
        attended, full_out, preferred_element_type=jnp.float32
    )
    inv_rms = lax.rsqrt(jnp.mean(hidden * hidden, axis=-1, keepdims=True) + epsilon)
    unit_rows = hidden * inv_rms
    normed = (unit_rows * norm_gain).astype(jnp.bfloat16)
    expert_of = expert_ids[:, 0]
    onehot = (expert_of[:, None] == jnp.arange(experts, dtype=jnp.int32)[None, :]).astype(
        jnp.bfloat16
    )
    row_iota = jnp.arange(tokens_here, dtype=jnp.int32)
    earlier_mask = (row_iota[:, None] > row_iota[None, :]).astype(jnp.bfloat16)
    earlier = jnp.dot(earlier_mask, onehot, preferred_element_type=jnp.float32)
    rank_index = jnp.sum(earlier * onehot.astype(jnp.float32), axis=1).astype(jnp.int32)
    slot_index = expert_of * capacity + rank_index
    empty_rows = jnp.zeros((experts * capacity, D), jnp.bfloat16)
    send_buffer = empty_rows.at[slot_index].set(normed).reshape(experts, capacity, D)
    gate_local = gate_weight[0]
    up_local = up_weight[0]
    down_local = down_weight[0]
    block_width = FF // data_ways
    arrived = lax.all_to_all(send_buffer, "expert", split_axis=0, concat_axis=0, tiled=True)
    piece_rows = arrived.shape[1]
    gathered = lax.all_gather(arrived, "dp", axis=0, tiled=True)
    flattened = gathered.reshape(-1, D)
    gate_pre = jnp.dot(flattened, gate_local, preferred_element_type=jnp.float32)
    up_pre = jnp.dot(flattened, up_local, preferred_element_type=jnp.float32)
    activated = (jax.nn.silu(gate_pre) * up_pre).astype(jnp.bfloat16)
    partial_out = jnp.dot(activated, down_local, preferred_element_type=jnp.float32)
    summed = lax.psum_scatter(
        partial_out.reshape(data_ways * experts, piece_rows, D).astype(jnp.bfloat16),
        "dp",
        scatter_dimension=0,
        tiled=True,
    )
    returned = lax.all_to_all(summed, "expert", split_axis=0, concat_axis=0, tiled=True)
    gate_saved = gate_pre.reshape(data_ways * experts, piece_rows, block_width)
    up_saved = up_pre.reshape(data_ways * experts, piece_rows, block_width)
    expert_back = returned.reshape(experts * capacity, D)[slot_index]
    layer_out = (hidden + expert_back.astype(jnp.float32)).astype(jnp.bfloat16)
    grad_buffer = empty_rows.at[slot_index].set(out_grad).reshape(experts, capacity, D)
    grad_arrived = lax.all_to_all(grad_buffer, "expert", split_axis=0, concat_axis=0, tiled=True)
    grad_gathered = lax.all_gather(grad_arrived, "dp", axis=0, tiled=True)
    grad_flat = grad_gathered.reshape(-1, D)
    gate_pre = gate_saved.reshape(-1, block_width)
    up_pre = up_saved.reshape(-1, block_width)
    sigmoid_gate = jax.nn.sigmoid(gate_pre)
    grad_act = contract_last(grad_flat, down_local)
    grad_gate = (grad_act * up_pre * sigmoid_gate * (1.0 + gate_pre * (1.0 - sigmoid_gate))).astype(
        jnp.bfloat16
    )
    grad_up = (grad_act * jax.nn.silu(gate_pre)).astype(jnp.bfloat16)
    partial_grad = contract_last(grad_gate, gate_local) + contract_last(grad_up, up_local)
    grad_normed_rows = lax.psum_scatter(
        partial_grad.reshape(data_ways * experts, capacity, D).astype(jnp.bfloat16),
        "dp",
        scatter_dimension=0,
        tiled=True,
    )
    grad_returned = lax.all_to_all(
        grad_normed_rows, "expert", split_axis=0, concat_axis=0, tiled=True
    )
    grad_normed = grad_returned.reshape(experts * capacity, D)[slot_index].astype(jnp.float32)
    scaled = grad_normed * norm_gain
    resid_grad = (
        out_grad.astype(jnp.float32)
        + inv_rms * (scaled - unit_rows * jnp.mean(scaled * unit_rows, axis=-1, keepdims=True))
    ).astype(jnp.bfloat16)
    grad_shard = lax.psum_scatter(
        contract_first(attended, resid_grad).astype(jnp.bfloat16),
        "expert",
        scatter_dimension=0,
        tiled=True,
    )
    weight_grad = lax.psum(grad_shard, ("section", "dp")).astype(jnp.float32)
    grad_attended = contract_last(resid_grad, full_out).astype(jnp.bfloat16)
    grad_heads = grad_attended.reshape(tokens_here, HEADS, HEAD)
    grad_probs = jnp.einsum(
        "thd,shd->hts", grad_heads, value_heads, preferred_element_type=jnp.float32
    )
    row_delta = jnp.sum(attn_probs * grad_probs, axis=-1, keepdims=True)
    grad_scores = (attn_probs * (grad_probs - row_delta)).astype(jnp.bfloat16)
    query_grad = (
        (
            jnp.einsum("hts,shd->thd", grad_scores, key_heads, preferred_element_type=jnp.float32)
            * inv_root
        )
        .reshape(tokens_here, A)
        .astype(jnp.bfloat16)
    )
    key_part = (
        jnp.einsum("hts,thd->shd", grad_scores, query_heads, preferred_element_type=jnp.float32)
        * inv_root
    )
    value_part = jnp.einsum(
        "hts,thd->shd", probs_low, grad_heads, preferred_element_type=jnp.float32
    )
    key_value = lax.psum_scatter(
        jnp.concatenate(
            [
                key_part.reshape(lax.axis_size("dp") * tokens_here, A),
                value_part.reshape(lax.axis_size("dp") * tokens_here, A),
            ],
            axis=1,
        ).astype(jnp.bfloat16),
        "dp",
        scatter_dimension=0,
        tiled=True,
    ).astype(jnp.float32)
    key_grad = key_value[:, :A].astype(jnp.bfloat16)
    value_grad = key_value[:, A:].astype(jnp.bfloat16)
    return (layer_out, resid_grad, query_grad, key_grad, value_grad, weight_grad)


def solution(mesh):
    return jax.shard_map(
        shards,
        mesh=mesh,
        in_specs=(
            P(("section", "expert", "dp"), None),
            P(("section", "expert", "dp"), None),
            P(("section", "expert", "dp"), None),
            P(("section", "expert", "dp"), None),
            P("expert", None),
            P(),
            P("expert", None, "dp"),
            P("expert", None, "dp"),
            P("expert", "dp", None),
            P(("section", "expert", "dp"), None),
            P(("section", "expert", "dp"), None),
        ),
        out_specs=(
            P(("section", "expert", "dp"), None),
            P(("section", "expert", "dp"), None),
            P(("section", "expert", "dp"), None),
            P(("section", "expert", "dp"), None),
            P(("section", "expert", "dp"), None),
            P("expert", None),
        ),
        check_vma=False,
    )
```

profile of v0, /device:TPU:0, one launch (start us, length us, event | category | flops | bytes accessed | tf_op | source)
XLA Modules:
  0.0 544.3 jit_solution(3329325886076428349)
XLA Ops:
  13.2 15.7 %all-gather.8.cloned.1.call-done = bf16[512,1024]{1,0:T(8,128)(2,1)} async-done(((bf16[128,1024]{1,0:T(8,128)(2,1)}), bf16[512,1024]{1,0:T(8,128)(2,1)}) %all-gather.8.cloned.1.call-update) | async-done | bytes 1048592 | tf_op jit(solution)/shard_map/all_gather | solution.py:47
  30.5 17.5 %all-gather.6.cloned.1.call-done = bf16[512,1024]{0,1:T(8,128)(2,1)} async-done(((bf16[128,1024]{0,1:T(8,128)(2,1)}), bf16[512,1024]{0,1:T(8,128)(2,1)}) %all-gather.6.cloned.1.call-update) | async-done | bytes 1048592 | tf_op jit(solution)/shard_map/all_gather | solution.py:46
  51.5 78.8 %all-gather.10.cloned.1.call-done = bf16[1024,2048]{1,0:T(8,128)(2,1)} async-done(((bf16[256,2048]{1,0:T(8,128)(2,1)}), bf16[1024,2048]{1,0:T(8,128)(2,1)}) %all-gather.10.cloned.1.call-update) | async-done | bytes 4194320 | tf_op jit(solution)/shard_map/all_gather | solution.py:65
  130.3 3.2 multiply_reduce_fusion.3
  135.3 29.0 %all_to_all.20 = bf16[4,64,2048]{2,1,0:T(8,128)(2,1)} all-to-all(bf16[4,64,2048]{2,1,0:T(8,128)(2,1)S(1)} %bitcast.80), channel_id=1, replica_groups=mesh['section'=2,'expert'=4,'dp'=4] {'expert'}, dimensions={0} | all-to-all | bytes 2097152 | tf_op jit(solution)/shard_map/all_to_all | solution.py:87
  166.6 28.4 %all_to_all.21 = bf16[4,64,2048]{2,1,0:T(8,128)(2,1)} all-to-all(bf16[4,64,2048]{2,1,0:T(8,128)(2,1)S(1)} %bitcast.78), channel_id=1, replica_groups=mesh['section'=2,'expert'=4,'dp'=4] {'expert'}, dimensions={0} | all-to-all | bytes 2097152 | tf_op jit(solution)/shard_map/all_to_all | solution.py:107
  195.1 2.9 all-gather.12.cloned.1.call-done
  198.0 7.6 %fusion.11 = f32[1024,1024]{1,0:T(8,128)S(1)} fusion(bf16[1024,2048]{1,0:T(8,128)(2,1)} %bitcast.94, bf16[1,2048,1024]{2,1,0:T(8,128)(2,1)} %param.17), kind=kOutput, calls=%fused_computation.16 | convolution fusion | flops 4294967296 | bytes 12582912 | tf_op jit(solution)/shard_map/dot_general | solution.py:91
  205.7 6.5 %multiply_convert_fusion.2 = (bf16[1024,1024]{1,0:T(8,128)(2,1)S(1)}, f32[1024,1024]{1,0:T(8,128)}) fusion(f32[1024,1024]{1,0:T(8,128)S(1)} %fusion.11, bf16[1024,2048]{1,0:T(8,128)(2,1)S(1)} %bitcast.95, bf16[1,2048,1024]{2,1,0:T(8,128)(2,1)S(1)} %copy-done.10), kind=kOutput, calls=%fused_computation.20 | convolution fusion | flops 4301258752 | bytes 18874368 | tf_op jit(solution)/shard_map/dot_general | solution.py:92
  212.2 6.1 %fusion.14 = bf16[16,64,2048]{2,1,0:T(8,128)(2,1)} fusion(bf16[16,64,1024]{2,1,0:T(8,128)(2,1)S(1)} %bitcast.97, bf16[1,1024,2048]{2,1,0:T(8,128)(2,1)S(1)} %copy-done.9), kind=kOutput, calls=%fused_computation.24 | convolution fusion | flops 4297064448 | bytes 10485760 | tf_op jit(solution)/shard_map/dot_general | solution.py:94
  218.6 15.3 %all-gather.14.cloned.1.call-done = bf16[16,64,2048]{2,1,0:T(8,128)(2,1)} async-done(((bf16[4,64,2048]{2,1,0:T(8,128)(2,1)}), bf16[16,64,2048]{2,1,0:T(8,128)(2,1)}) %all-gather.14.cloned.1.call-update) | async-done | bytes 4194320 | tf_op jit(solution)/shard_map/all_gather | solution.py:108
  233.9 7.7 %fusion.3 = f32[1024,1024]{1,0:T(8,128)S(1)} fusion(bf16[1024,2048]{1,0:T(8,128)(2,1)} %bitcast.93, bf16[1,1024,2048]{2,1,0:T(8,128)(2,1)} %param.19), kind=kOutput, calls=%fused_computation.8 | convolution fusion | flops 4294967296 | bytes 12582912 | tf_op jit(solution)/shard_map/dot_general | solution.py:16
  241.7 6.9 %fusion.5 = f32[1024,2048]{1,0:T(8,128)} fusion(bf16[1,2048,1024]{2,1,0:T(8,128)(2,1)S(1)} %copy-done.11, f32[1024,1024]{1,0:T(8,128)S(1)} %fusion.3, f32[1024,1024]{1,0:T(8,128)S(1)} %copy-done.15), kind=kOutput, calls=%fused_computation.10 | convolution fusion | flops 4301258752 | bytes 20971520 | tf_op jit(solution)/shard_map/dot_general | solution.py:16
  248.5 14.3 %add_convert_fusion = bf16[1024,2048]{1,0:T(8,128)(2,1)} fusion(f32[1024,2048]{1,0:T(8,128)} %fusion.5, bf16[1,2048,1024]{2,1,0:T(8,128)(2,1)S(1)} %copy-done.12, f32[1024,1024]{1,0:T(8,128)} %copy-done.14, f32[1024,1024]{1,0:T(8,128)} %copy-done.16, f32[1024,1024]{1,0:T(8,128)} %get-tuple-element.33), kind=kOutput, calls=%fused_computation.5 | convolution fusion | flops 4309647360 | bytes 29360128 | tf_op jit(solution)/shard_map/dot_general | solution.py:16
  262.9 18.0 %reduce-scatter.5.cloned.1.call-done = bf16[4,64,2048]{2,1,0:T(8,128)(2,1)} async-done(((bf16[16,64,2048]{2,1,0:T(8,128)(2,1)}), bf16[4,64,2048]{2,1,0:T(8,128)(2,1)}) %reduce-scatter.5.cloned.1.call-update) | async-done | bytes 1048592 | tf_op jit(solution)/shard_map/reduce_scatter | solution.py:95
  280.9 4.6 all-to-all-start.1
  285.5 42.6 %reduce-scatter.7.cloned.1.call-done = bf16[4,64,2048]{2,1,0:T(8,128)(2,1)} async-done(((bf16[16,64,2048]{2,1,0:T(8,128)(2,1)}), bf16[4,64,2048]{2,1,0:T(8,128)(2,1)}) %reduce-scatter.7.cloned.1.call-update) | async-done | bytes 1048592 | tf_op jit(solution)/shard_map/reduce_scatter | solution.py:119
  328.1 4.6 all-to-all-start.3
  334.4 23.8 %all-to-all-done.3 = bf16[4,64,2048]{2,1,0:T(8,128)(2,1)S(1)} async-done(((bf16[4,64,2048]{2,1,0:T(8,128)(2,1)}), bf16[4,64,2048]{2,1,0:T(8,128)(2,1)S(1)}, u32[]{:S(2)}, u32[]{:S(2)}) %all-to-all-start.3) | async-done | bytes 1048608 | tf_op jit(solution)/shard_map/all_to_all | solution.py:125
  361.9 3.2 convolution_convert_fusion
  365.3 3.9 convolution_convert_fusion.3
  381.5 58.7 %reduce-scatter.11.cloned.1.call-done = bf16[256,2048]{1,0:T(8,128)(2,1)} async-done(((bf16[1024,2048]{1,0:T(8,128)(2,1)}), bf16[256,2048]{1,0:T(8,128)(2,1)}) %reduce-scatter.11.cloned.1.call-update) | async-done | bytes 1048592 | tf_op jit(solution)/shard_map/reduce_scatter | solution.py:134
  441.5 33.5 %reduce-scatter.9.cloned.1.call-done = bf16[128,2048]{1,0:T(8,128)(2,1)} async-done(((bf16[512,2048]{1,0:T(8,128)(2,1)}), bf16[128,2048]{1,0:T(8,128)(2,1)}) %reduce-scatter.9.cloned.1.call-update) | async-done | bytes 524304 | tf_op jit(solution)/shard_map/reduce_scatter | solution.py:163
  476.8 57.9 %all-reduce.2.cloned.1.call-done = bf16[256,2048]{1,0:T(8,128)(2,1)} async-done(((bf16[256,2048]{1,0:T(8,128)(2,1)}), bf16[256,2048]{1,0:T(8,128)(2,1)}) %all-reduce.2.cloned.1.call-update) | async-done | bytes 1048592 | tf_op jit(solution)/shard_map/psum | solution.py:140
  (83 shorter events, 39.2 us)
Async XLA Ops:
  7.2 21.8 %all-gather.8.cloned.1.call-start = ((), (), s32[]{:S(2)}) async-start(), calls=%async_computation.9 | async-start | bytes 1310720 | tf_op jit(solution)/shard_map/all_gather | solution.py:47
  7.9 40.1 %all-gather.6.cloned.1.call-start = ((), (), s32[]{:S(2)}) async-start(), calls=%async_computation.8 | async-start | bytes 1310720 | tf_op jit(solution)/shard_map/all_gather | solution.py:46
  9.8 120.6 %all-gather.10.cloned.1.call-start = ((), (), s32[]{:S(2)}) async-start(), calls=%async_computation.10 | async-start | bytes 5242880 | tf_op jit(solution)/shard_map/all_gather | solution.py:65
  10.5 187.5 %all-gather.12.cloned.1.call-start = ((), (), s32[]{:S(2)}) async-start(), calls=%async_computation.11 | async-start | bytes 5242880 | tf_op jit(solution)/shard_map/all_gather | solution.py:89
  30.5 21.0 %copy-start.6 = (bf16[512,1024]{0,1:T(8,128)(2,1)}, bf16[512,1024]{0,1:T(8,128)(2,1)S(1)}, u32[]{:S(2)}) copy-start(bf16[512,1024]{0,1:T(8,128)(2,1)S(1)} %copy.41) | copy-start | bytes 3145732
  51.5 82.0 %copy-start.8 = (f32[2048]{0:T(1024)S(1)}, f32[2048]{0:T(1024)}, u32[]{:S(2)}) copy-start(f32[2048]{0:T(1024)} %param.16) | copy-start | bytes 24580
  164.4 69.5 %all-gather.14.cloned.1.call-start = ((), (), s32[]{:S(2)}) async-start(), calls=%async_computation.13 | async-start | bytes 5242880 | tf_op jit(solution)/shard_map/all_gather | solution.py:108
  195.1 85.8 %reduce-scatter.5.cloned.1.call-start = ((), (), s32[]{:S(2)}) async-start(), calls=%async_computation.12 | async-start | bytes 5242880 | tf_op jit(solution)/shard_map/reduce_scatter | solution.py:95
  198.0 7.7 %copy-start.10 = (bf16[1,2048,1024]{2,1,0:T(8,128)(2,1)S(1)}, bf16[1,2048,1024]{2,1,0:T(8,128)(2,1)}, u32[]{:S(2)}) copy-start(bf16[1,2048,1024]{2,1,0:T(8,128)(2,1)} %param.18) | copy-start | bytes 12582916
  198.0 7.7 %copy-start.13 = (bf16[16,64,2048]{2,1,0:T(8,128)(2,1)S(1)}, bf16[16,64,2048]{2,1,0:T(8,128)(2,1)}, u32[]{:S(2)}) copy-start(bf16[16,64,2048]{2,1,0:T(8,128)(2,1)} %all-gather.12.cloned.1.call-done) | copy-start | bytes 12582916
  205.7 6.6 %copy-start.14 = (f32[1024,1024]{1,0:T(8,128)}, f32[1024,1024]{1,0:T(8,128)S(1)}, u32[]{:S(2)}) copy-start(f32[1024,1024]{1,0:T(8,128)S(1)} %fusion.11) | copy-start | bytes 12582916
  205.7 6.6 %copy-start.9 = (bf16[1,1024,2048]{2,1,0:T(8,128)(2,1)S(1)}, bf16[1,1024,2048]{2,1,0:T(8,128)(2,1)}, u32[]{:S(2)}) copy-start(bf16[1,1024,2048]{2,1,0:T(8,128)(2,1)} %param.19) | copy-start | bytes 12582916
  218.4 109.7 %reduce-scatter.7.cloned.1.call-start = ((), (), s32[]{:S(2)}) async-start(), calls=%async_computation.14 | async-start | bytes 5242880 | tf_op jit(solution)/shard_map/reduce_scatter | solution.py:119
  233.9 7.7 %copy-start.11 = (bf16[1,2048,1024]{2,1,0:T(8,128)(2,1)S(1)}, bf16[1,2048,1024]{2,1,0:T(8,128)(2,1)}, u32[]{:S(2)}) copy-start(bf16[1,2048,1024]{2,1,0:T(8,128)(2,1)} %param.18) | copy-start | bytes 12582916
  233.9 7.7 %copy-start.15 = (f32[1024,1024]{1,0:T(8,128)S(1)}, f32[1024,1024]{1,0:T(8,128)}, u32[]{:S(2)}) copy-start(f32[1024,1024]{1,0:T(8,128)} %copy-done.14) | copy-start | bytes 12582916
  241.7 6.9 %copy-start.16 = (f32[1024,1024]{1,0:T(8,128)}, f32[1024,1024]{1,0:T(8,128)S(1)}, u32[]{:S(2)}) copy-start(f32[1024,1024]{1,0:T(8,128)S(1)} %fusion.3) | copy-start | bytes 12582916
  241.7 6.9 %copy-start.12 = (bf16[1,2048,1024]{2,1,0:T(8,128)(2,1)S(1)}, bf16[1,2048,1024]{2,1,0:T(8,128)(2,1)}, u32[]{:S(2)}) copy-start(bf16[1,2048,1024]{2,1,0:T(8,128)(2,1)} %param.17) | copy-start | bytes 12582916
  280.9 47.2 %all-to-all-start.1 = ((bf16[4,64,2048]{2,1,0:T(8,128)(2,1)}), bf16[4,64,2048]{2,1,0:T(8,128)(2,1)S(1)}, u32[]{:S(2)}, u32[]{:S(2)}) async-start(bf16[4,64,2048]{2,1,0:T(8,128)(2,1)} %reduce-scatter.5.cloned.1.call-done), calls=%async_computation.2 | async-start | bytes 2097152 | tf_op jit(solution)/shard_map/all_to_all | solution.py:101
  328.1 30.1 %all-to-all-start.3 = ((bf16[4,64,2048]{2,1,0:T(8,128)(2,1)}), bf16[4,64,2048]{2,1,0:T(8,128)(2,1)S(1)}, u32[]{:S(2)}, u32[]{:S(2)}) async-start(bf16[4,64,2048]{2,1,0:T(8,128)(2,1)} %reduce-scatter.7.cloned.1.call-done), calls=%async_computation.5 | async-start | bytes 2097152 | tf_op jit(solution)/shard_map/all_to_all | solution.py:125
  332.7 107.5 %reduce-scatter.11.cloned.1.call-start = ((), (), s32[]{:S(2)}) async-start(), calls=%async_computation.16 | async-start | bytes 5242880 | tf_op jit(solution)/shard_map/reduce_scatter | solution.py:134
  365.0 5.0 copy-start.1
  365.1 109.9 %reduce-scatter.9.cloned.1.call-start = ((), (), s32[]{:S(2)}) async-start(), calls=%async_computation.15 | async-start | bytes 2621440 | tf_op jit(solution)/shard_map/reduce_scatter | solution.py:163
  378.5 61.6 %copy-start.3 = (bf16[512,1024]{0,1:T(8,128)(2,1)S(1)}, bf16[512,1024]{0,1:T(8,128)(2,1)}, u32[]{:S(2)}) copy-start(bf16[512,1024]{0,1:T(8,128)(2,1)} %all-gather.6.cloned.1.call-done) | copy-start | bytes 3145732
  381.4 153.3 %all-reduce.2.cloned.1.call-start = ((), (), s32[]{:S(2)}) async-start(), calls=%async_computation.17 | async-start | bytes 2097152 | tf_op jit(solution)/shard_map/psum | solution.py:140
  (5 other events, 14.2 us)
Sparse Core Ops, SparseCore 0:
  9.5 19.4 all-gather.7
  31.1 16.8 all-gather.5
  49.5 80.7 all-gather.9
  164.5 33.4 all-gather.11
  199.4 34.4 all-gather.13
  236.3 44.5 reduce-scatter.4
  283.4 44.5 reduce-scatter.6
  365.2 74.9 reduce-scatter.10
  443.2 31.6 reduce-scatter.8
  478.0 56.6 all-reduce.1
where the time goes:
time: 545 us; the launch traced here: 544 us
  waiting for transfers between devices  366 us (67%)
  matrix products  68.7 us (13%)
  blocking collectives  57.4 us (11%)
  local copies, waits for them, and re-layouts  16.5 us (3%)
  between operations  14.4 us (3%)
  other arithmetic  11.2 us (2%)
  starting transfers between devices  9.97 us (2%)
    all_gather x1, waiting for transfers between devices, shards(): full_out = lax.all_gather(out_weight, 'expert', axis=0, tiled=True)  78.8 us
    reduce_scatter x1, waiting for transfers between devices, shards(): lax.psum_scatter(contract_first(attended, resid_grad).astype(jnp.bfloat16...  58.7 us
    psum x1, waiting for transfers between devices, shards(): weight_grad = lax.psum(grad_shard, ('section', 'dp')).astype(jnp.float32)  57.9 us
    reduce_scatter x1, waiting for transfers between devices, shards(): lax.psum_scatter(partial_grad.reshape(data_ways * experts, capacity, D).a...  42.6 us
    reduce_scatter x1, waiting for transfers between devices, shards(): lax.psum_scatter(jnp.concatenate([key_part.reshape(lax.axis_size('dp') *...  33.5 us
    dot_general x4, matrix products, contract_last(): lax.dot_general(left_side, right_side, (((1,), (1,)), ((), ())), preferre...  32.7 us
    all_to_all x1, blocking collectives, shards(): lax.all_to_all(send_buffer, 'expert', split_axis=0, concat_axis=0, tiled=...  29 us
    all_to_all x1, blocking collectives, shards(): lax.all_to_all(grad_buffer, 'expert', split_axis=0, concat_axis=0, tiled=...  28.4 us
  transfers between devices with their start and end apart: 12, of which 11 were waited for; matrix products, arithmetic and copies ran while one was open for 15% of the time, Pallas kernels for 0%

commit v1 on v0

--- a/solution.py
+++ b/solution.py
@@ -62,7 +62,14 @@
         .reshape(tokens_here, A)
         .astype(jnp.bfloat16)
     )
-    full_out = lax.all_gather(out_weight, "expert", axis=0, tiled=True)
+    ring = [out_weight]
+    for hop in range(3):
+        ring.append(lax.ppermute(ring[-1], "expert", [(dev, (dev + 1) % 4) for dev in range(4)]))
+    full_out = jnp.roll(
+        jnp.concatenate(ring[::-1], axis=0),
+        (lax.axis_index("expert") + 1) * ring[0].shape[0],
+        axis=0,
+    )
     hidden = residual.astype(jnp.float32) + jnp.dot(
         attended, full_out, preferred_element_type=jnp.float32
     )

time: 545 us -> 507 us (0.930)
  waiting for transfers between devices: 366 us -> 319 us
  local copies, waits for them, and re-layouts: 16.5 us -> 27.5 us
    all_gather x1 -> x0, waiting for transfers between devices: 78.8 us -> none  [shards(): full_out = lax.all_gather(out_weight, 'expert', axis=0, tiled=True)]
    ppermute x0 -> x3, waiting for transfers between devices: none -> 65.7 us  [shards(): lax.ppermute(ring[-1], 'expert', [(dev, (dev + 1) % 4) for dev in range(4)])]
    all_gather x1, waiting for transfers between devices: 17.5 us -> 0.01 us  [shards(): lax.all_gather(attn_keys, 'dp', axis=0, tiled=True)]
    all_gather x1, waiting for transfers between devices: 15.7 us -> 0.01 us  [shards(): lax.all_gather(attn_values, 'dp', axis=0, tiled=True)]
    unnamed x36 -> x53, local copies, waits for them, and re-layouts: 2.72 us -> 12.9 us
  transfers between devices with their start and end apart: 12 -> 14, of which waited for: 11 -> 11; matrix products, arithmetic and copies ran while one was open for 15% -> 16% of each run, Pallas kernels for 0% -> 0%
where the time goes in v1:
time: 507 us; the launch traced here: 506 us
  waiting for transfers between devices  319 us (63%)
  matrix products  67.2 us (13%)
  blocking collectives  54.6 us (11%)
  local copies, waits for them, and re-layouts  27.5 us (5%)
  between operations  14.2 us (3%)
  starting transfers between devices  13.3 us (3%)
  other arithmetic  11 us (2%)
    ppermute x3, waiting for transfers between devices, shards(): lax.ppermute(ring[-1], 'expert', [(dev, (dev + 1) % 4) for dev in range(4)])  65.7 us
    reduce_scatter x1, waiting for transfers between devices, shards(): lax.psum_scatter(contract_first(attended, resid_grad).astype(jnp.bfloat16...  58.1 us
    psum x1, waiting for transfers between devices, shards(): weight_grad = lax.psum(grad_shard, ('section', 'dp')).astype(jnp.float32)  58.1 us
    reduce_scatter x1, waiting for transfers between devices, shards(): lax.psum_scatter(partial_grad.reshape(data_ways * experts, capacity, D).a...  42.4 us
    reduce_scatter x1, waiting for transfers between devices, shards(): lax.psum_scatter(jnp.concatenate([key_part.reshape(lax.axis_size('dp') *...  33.5 us
    dot_general x4, matrix products, contract_last(): lax.dot_general(left_side, right_side, (((1,), (1,)), ((), ())), preferre...  32.5 us
    all_to_all x1, blocking collectives, shards(): lax.all_to_all(grad_buffer, 'expert', split_axis=0, concat_axis=0, tiled=...  27.8 us
    all_to_all x1, blocking collectives, shards(): lax.all_to_all(send_buffer, 'expert', split_axis=0, concat_axis=0, tiled=...  26.9 us
  transfers between devices with their start and end apart: 14, of which 11 were waited for; matrix products, arithmetic and copies ran while one was open for 16% of the time, Pallas kernels for 0%

profile of v1, /device:TPU:0, one launch (start us, length us, event | category | flops | bytes accessed | tf_op | source)
XLA Modules:
  0.0 506.4 jit_solution(11769580457773176613)
XLA Ops:
  7.9 3.1 collective-permute-start
  12.9 23.5 %collective-permute-done = bf16[256,2048]{1,0:T(8,128)(2,1)S(1)} collective-permute-done((bf16[256,2048]{1,0:T(8,128)(2,1)}, bf16[256,2048]{1,0:T(8,128)(2,1)S(1)}, u32[]{:S(2)}, u32[]{:S(2)}) %collective-permute-start) | collective-permute-done | bytes 1048608 | tf_op jit(solution)/shard_map/ppermute | solution.py:67
  37.6 25.1 %collective-permute-done.1 = bf16[256,2048]{1,0:T(8,128)(2,1)} collective-permute-done((bf16[256,2048]{1,0:T(8,128)(2,1)S(1)}, bf16[256,2048]{1,0:T(8,128)(2,1)}, u32[]{:S(2)}, u32[]{:S(2)}) %collective-permute-start.1) | collective-permute-done | bytes 1048608 | tf_op jit(solution)/shard_map/ppermute | solution.py:67
  71.2 17.0 %collective-permute-done.2 = bf16[256,2048]{1,0:T(8,128)(2,1)} collective-permute-done((bf16[256,2048]{1,0:T(8,128)(2,1)}, bf16[256,2048]{1,0:T(8,128)(2,1)}, u32[]{:S(2)}, u32[]{:S(2)}) %collective-permute-start.2) | collective-permute-done | bytes 1048608 | tf_op jit(solution)/shard_map/ppermute | solution.py:67
  93.9 3.2 copy-done
  99.7 26.9 %all_to_all.20 = bf16[4,64,2048]{2,1,0:T(8,128)(2,1)} all-to-all(bf16[4,64,2048]{2,1,0:T(8,128)(2,1)S(1)} %bitcast.78), channel_id=1, replica_groups=mesh['section'=2,'expert'=4,'dp'=4] {'expert'}, dimensions={0} | all-to-all | bytes 2097152 | tf_op jit(solution)/shard_map/all_to_all | solution.py:94
  128.9 27.8 %all_to_all.21 = bf16[4,64,2048]{2,1,0:T(8,128)(2,1)} all-to-all(bf16[4,64,2048]{2,1,0:T(8,128)(2,1)S(1)} %bitcast.76), channel_id=1, replica_groups=mesh['section'=2,'expert'=4,'dp'=4] {'expert'}, dimensions={0} | all-to-all | bytes 2097152 | tf_op jit(solution)/shard_map/all_to_all | solution.py:114
  159.7 7.6 %fusion.11 = f32[1024,1024]{1,0:T(8,128)S(1)} fusion(bf16[1024,2048]{1,0:T(8,128)(2,1)} %bitcast.92, bf16[1,2048,1024]{2,1,0:T(8,128)(2,1)} %param.17), kind=kOutput, calls=%fused_computation.16 | convolution fusion | flops 4294967296 | bytes 12582912 | tf_op jit(solution)/shard_map/dot_general | solution.py:98
  167.4 6.5 %multiply_convert_fusion.2 = (bf16[1024,1024]{1,0:T(8,128)(2,1)S(1)}, f32[1024,1024]{1,0:T(8,128)}) fusion(f32[1024,1024]{1,0:T(8,128)S(1)} %fusion.11, bf16[1024,2048]{1,0:T(8,128)(2,1)S(1)} %bitcast.93, bf16[1,2048,1024]{2,1,0:T(8,128)(2,1)S(1)} %copy-done.15), kind=kOutput, calls=%fused_computation.20 | convolution fusion | flops 4301258752 | bytes 18874368 | tf_op jit(solution)/shard_map/dot_general | solution.py:99
  173.9 6.1 %fusion.14 = bf16[16,64,2048]{2,1,0:T(8,128)(2,1)} fusion(bf16[16,64,1024]{2,1,0:T(8,128)(2,1)S(1)} %bitcast.95, bf16[1,1024,2048]{2,1,0:T(8,128)(2,1)S(1)} %copy-done.14), kind=kOutput, calls=%fused_computation.24 | convolution fusion | flops 4297064448 | bytes 10485760 | tf_op jit(solution)/shard_map/dot_general | solution.py:101
  180.3 15.3 %all-gather.11.cloned.1.call-done = bf16[16,64,2048]{2,1,0:T(8,128)(2,1)} async-done(((bf16[4,64,2048]{2,1,0:T(8,128)(2,1)}), bf16[16,64,2048]{2,1,0:T(8,128)(2,1)}) %all-gather.11.cloned.1.call-update) | async-done | bytes 4194320 | tf_op jit(solution)/shard_map/all_gather | solution.py:115
  195.6 7.7 %fusion.3 = f32[1024,1024]{1,0:T(8,128)S(1)} fusion(bf16[1024,2048]{1,0:T(8,128)(2,1)} %bitcast.91, bf16[1,1024,2048]{2,1,0:T(8,128)(2,1)} %param.19), kind=kOutput, calls=%fused_computation.8 | convolution fusion | flops 4294967296 | bytes 12582912 | tf_op jit(solution)/shard_map/dot_general | solution.py:16
  203.4 6.7 %fusion.5 = f32[1024,2048]{1,0:T(8,128)} fusion(bf16[1,2048,1024]{2,1,0:T(8,128)(2,1)S(1)} %copy-done.16, f32[1024,1024]{1,0:T(8,128)S(1)} %fusion.3, f32[1024,1024]{1,0:T(8,128)S(1)} %copy-done.20), kind=kOutput, calls=%fused_computation.10 | convolution fusion | flops 4301258752 | bytes 20971520 | tf_op jit(solution)/shard_map/dot_general | solution.py:16
  210.1 14.3 %add_convert_fusion = bf16[1024,2048]{1,0:T(8,128)(2,1)} fusion(f32[1024,2048]{1,0:T(8,128)} %fusion.5, bf16[1,2048,1024]{2,1,0:T(8,128)(2,1)S(1)} %copy-done.17, f32[1024,1024]{1,0:T(8,128)} %copy-done.19, f32[1024,1024]{1,0:T(8,128)} %copy-done.21, f32[1024,1024]{1,0:T(8,128)} %get-tuple-element.33), kind=kOutput, calls=%fused_computation.5 | convolution fusion | flops 4309647360 | bytes 29360128 | tf_op jit(solution)/shard_map/dot_general | solution.py:16
  224.5 18.1 %reduce-scatter.5.cloned.1.call-done = bf16[4,64,2048]{2,1,0:T(8,128)(2,1)} async-done(((bf16[16,64,2048]{2,1,0:T(8,128)(2,1)}), bf16[4,64,2048]{2,1,0:T(8,128)(2,1)}) %reduce-scatter.5.cloned.1.call-update) | async-done | bytes 1048592 | tf_op jit(solution)/shard_map/reduce_scatter | solution.py:102
  242.6 4.6 all-to-all-start.1
  247.2 42.4 %reduce-scatter.7.cloned.1.call-done = bf16[4,64,2048]{2,1,0:T(8,128)(2,1)} async-done(((bf16[16,64,2048]{2,1,0:T(8,128)(2,1)}), bf16[4,64,2048]{2,1,0:T(8,128)(2,1)}) %reduce-scatter.7.cloned.1.call-update) | async-done | bytes 1048592 | tf_op jit(solution)/shard_map/reduce_scatter | solution.py:126
  289.6 4.6 all-to-all-start.3
  296.0 23.8 %all-to-all-done.3 = bf16[4,64,2048]{2,1,0:T(8,128)(2,1)S(1)} async-done(((bf16[4,64,2048]{2,1,0:T(8,128)(2,1)}), bf16[4,64,2048]{2,1,0:T(8,128)(2,1)S(1)}, u32[]{:S(2)}, u32[]{:S(2)}) %all-to-all-start.3) | async-done | bytes 1048608 | tf_op jit(solution)/shard_map/all_to_all | solution.py:132
  324.1 3.2 convolution_convert_fusion
  328.3 3.7 fusion.29
  344.2 58.1 %reduce-scatter.11.cloned.1.call-done = bf16[256,2048]{1,0:T(8,128)(2,1)} async-done(((bf16[1024,2048]{1,0:T(8,128)(2,1)}), bf16[256,2048]{1,0:T(8,128)(2,1)}) %reduce-scatter.11.cloned.1.call-update) | async-done | bytes 1048592 | tf_op jit(solution)/shard_map/reduce_scatter | solution.py:141
  403.7 33.5 %reduce-scatter.9.cloned.1.call-done = bf16[128,2048]{1,0:T(8,128)(2,1)} async-done(((bf16[512,2048]{1,0:T(8,128)(2,1)}), bf16[128,2048]{1,0:T(8,128)(2,1)}) %reduce-scatter.9.cloned.1.call-update) | async-done | bytes 524304 | tf_op jit(solution)/shard_map/reduce_scatter | solution.py:170
  439.0 58.1 %all-reduce.2.cloned.1.call-done = bf16[256,2048]{1,0:T(8,128)(2,1)} async-done(((bf16[256,2048]{1,0:T(8,128)(2,1)}), bf16[256,2048]{1,0:T(8,128)(2,1)}) %all-reduce.2.cloned.1.call-update) | async-done | bytes 1048592 | tf_op jit(solution)/shard_map/psum | solution.py:147
  (104 shorter events, 51.1 us)
Async XLA Ops:
  7.2 57.1 %all-gather.7.cloned.1.call-start = ((), (), s32[]{:S(2)}) async-start(), calls=%async_computation.9 | async-start | bytes 1310720 | tf_op jit(solution)/shard_map/all_gather | solution.py:47
  7.9 58.6 %all-gather.5.cloned.1.call-start = ((), (), s32[]{:S(2)}) async-start(), calls=%async_computation.8 | async-start | bytes 1310720 | tf_op jit(solution)/shard_map/all_gather | solution.py:46
  7.9 28.5 %collective-permute-start = (bf16[256,2048]{1,0:T(8,128)(2,1)}, bf16[256,2048]{1,0:T(8,128)(2,1)S(1)}, u32[]{:S(2)}, u32[]{:S(2)}) collective-permute-start(bf16[256,2048]{1,0:T(8,128)(2,1)} %param.15), channel_id=1, source_target_pairs={{0,4},{4,8},{8,12},{12,0},{1,5},{5,9},{9,13},{13,1},{2,6},{6,10},{... | collective-permute-start | bytes 3145736 | tf_op jit(solution)/shard_map/ppermute | solution.py:67
  12.9 146.8 %all-gather.9.cloned.1.call-start = ((), (), s32[]{:S(2)}) async-start(), calls=%async_computation.10 | async-start | bytes 5242880 | tf_op jit(solution)/shard_map/all_gather | solution.py:96
  36.4 26.2 %collective-permute-start.1 = (bf16[256,2048]{1,0:T(8,128)(2,1)S(1)}, bf16[256,2048]{1,0:T(8,128)(2,1)}, u32[]{:S(2)}, u32[]{:S(2)}) collective-permute-start(bf16[256,2048]{1,0:T(8,128)(2,1)S(1)} %collective-permute-done), channel_id=1, source_target_pairs={{0,4},{4,8},{8,12},{12,0},{1,5},{5,9},{9,13},{13,1},{2,6},{6,10},{... | collective-permute-start | bytes 3145736 | tf_op jit(solution)/shard_map/ppermute | solution.py:67
  62.7 25.6 %collective-permute-start.2 = (bf16[256,2048]{1,0:T(8,128)(2,1)}, bf16[256,2048]{1,0:T(8,128)(2,1)}, u32[]{:S(2)}, u32[]{:S(2)}) collective-permute-start(bf16[256,2048]{1,0:T(8,128)(2,1)} %collective-permute-done.1), channel_id=1, source_target_pairs={{0,4},{4,8},{8,12},{12,0},{1,5},{5,9},{9,13},{13,1},{2,6},{6,10},{... | collective-permute-start | bytes 3145736 | tf_op jit(solution)/shard_map/ppermute | solution.py:67
  71.2 22.7 %copy-start.9 = (bf16[8,128,128]{1,2,0:T(8,128)(2,1)}, bf16[8,128,128]{1,2,0:T(8,128)(2,1)S(1)}, u32[]{:S(2)}) copy-start(bf16[8,128,128]{1,2,0:T(8,128)(2,1)S(1)} %convolution_convert_fusion.2) | copy-start | bytes 786436
  71.2 19.7 %copy-start.5 = (bf16[256,2048]{1,0:T(8,128)(2,1)S(1)}, bf16[256,2048]{1,0:T(8,128)(2,1)}, u32[]{:S(2)}) copy-start(bf16[256,2048]{1,0:T(8,128)(2,1)} %param.15) | copy-start | bytes 3145732
  126.6 69.0 %all-gather.11.cloned.1.call-start = ((), (), s32[]{:S(2)}) async-start(), calls=%async_computation.12 | async-start | bytes 5242880 | tf_op jit(solution)/shard_map/all_gather | solution.py:115
  156.7 85.9 %reduce-scatter.5.cloned.1.call-start = ((), (), s32[]{:S(2)}) async-start(), calls=%async_computation.11 | async-start | bytes 5242880 | tf_op jit(solution)/shard_map/reduce_scatter | solution.py:102
  159.7 7.7 %copy-start.15 = (bf16[1,2048,1024]{2,1,0:T(8,128)(2,1)S(1)}, bf16[1,2048,1024]{2,1,0:T(8,128)(2,1)}, u32[]{:S(2)}) copy-start(bf16[1,2048,1024]{2,1,0:T(8,128)(2,1)} %param.18) | copy-start | bytes 12582916
  159.7 7.7 %copy-start.18 = (bf16[16,64,2048]{2,1,0:T(8,128)(2,1)S(1)}, bf16[16,64,2048]{2,1,0:T(8,128)(2,1)}, u32[]{:S(2)}) copy-start(bf16[16,64,2048]{2,1,0:T(8,128)(2,1)} %all-gather.9.cloned.1.call-done) | copy-start | bytes 12582916
  180.1 109.5 %reduce-scatter.7.cloned.1.call-start = ((), (), s32[]{:S(2)}) async-start(), calls=%async_computation.13 | async-start | bytes 5242880 | tf_op jit(solution)/shard_map/reduce_scatter | solution.py:126
  195.6 7.7 %copy-start.16 = (bf16[1,2048,1024]{2,1,0:T(8,128)(2,1)S(1)}, bf16[1,2048,1024]{2,1,0:T(8,128)(2,1)}, u32[]{:S(2)}) copy-start(bf16[1,2048,1024]{2,1,0:T(8,128)(2,1)} %param.18) | copy-start | bytes 12582916
  195.6 7.7 %copy-start.20 = (f32[1024,1024]{1,0:T(8,128)S(1)}, f32[1024,1024]{1,0:T(8,128)}, u32[]{:S(2)}) copy-start(f32[1024,1024]{1,0:T(8,128)} %copy-done.19) | copy-start | bytes 12582916
  203.4 6.7 %copy-start.21 = (f32[1024,1024]{1,0:T(8,128)}, f32[1024,1024]{1,0:T(8,128)S(1)}, u32[]{:S(2)}) copy-start(f32[1024,1024]{1,0:T(8,128)S(1)} %fusion.3) | copy-start | bytes 12582916
  203.4 6.7 %copy-start.17 = (bf16[1,2048,1024]{2,1,0:T(8,128)(2,1)S(1)}, bf16[1,2048,1024]{2,1,0:T(8,128)(2,1)}, u32[]{:S(2)}) copy-start(bf16[1,2048,1024]{2,1,0:T(8,128)(2,1)} %param.17) | copy-start | bytes 12582916
  242.6 47.0 %all-to-all-start.1 = ((bf16[4,64,2048]{2,1,0:T(8,128)(2,1)}), bf16[4,64,2048]{2,1,0:T(8,128)(2,1)S(1)}, u32[]{:S(2)}, u32[]{:S(2)}) async-start(bf16[4,64,2048]{2,1,0:T(8,128)(2,1)} %reduce-scatter.5.cloned.1.call-done), calls=%async_computation.2 | async-start | bytes 2097152 | tf_op jit(solution)/shard_map/all_to_all | solution.py:108
  289.6 30.2 %all-to-all-start.3 = ((bf16[4,64,2048]{2,1,0:T(8,128)(2,1)}), bf16[4,64,2048]{2,1,0:T(8,128)(2,1)S(1)}, u32[]{:S(2)}, u32[]{:S(2)}) async-start(bf16[4,64,2048]{2,1,0:T(8,128)(2,1)} %reduce-scatter.7.cloned.1.call-done), calls=%async_computation.5 | async-start | bytes 2097152 | tf_op jit(solution)/shard_map/all_to_all | solution.py:132
  294.2 108.1 %reduce-scatter.11.cloned.1.call-start = ((), (), s32[]{:S(2)}) async-start(), calls=%async_computation.15 | async-start | bytes 5242880 | tf_op jit(solution)/shard_map/reduce_scatter | solution.py:141
  296.0 25.0 %copy-start.8 = (bf16[128,2048]{1,0:T(8,128)(2,1)S(1)}, bf16[128,2048]{1,0:T(8,128)(2,1)}, u32[]{:S(2)}) copy-start(bf16[128,2048]{1,0:T(8,128)(2,1)} %gather_fusion) | copy-start | bytes 1572868
  327.3 109.9 %reduce-scatter.9.cloned.1.call-start = ((), (), s32[]{:S(2)}) async-start(), calls=%async_computation.14 | async-start | bytes 2621440 | tf_op jit(solution)/shard_map/reduce_scatter | solution.py:170
  341.4 61.1 %copy-start.6 = (bf16[512,1024]{0,1:T(8,128)(2,1)S(1)}, bf16[512,1024]{0,1:T(8,128)(2,1)}, u32[]{:S(2)}) copy-start(bf16[512,1024]{0,1:T(8,128)(2,1)} %all-gather.5.cloned.1.call-done) | copy-start | bytes 3145732
  344.2 152.9 %all-reduce.2.cloned.1.call-start = ((), (), s32[]{:S(2)}) async-start(), calls=%async_computation.16 | async-start | bytes 2097152 | tf_op jit(solution)/shard_map/psum | solution.py:147
  (12 other events, 46.4 us)
Sparse Core Ops, SparseCore 0:
  9.5 19.4 all-gather.6
  31.1 16.8 all-gather.4
  126.8 32.9 all-gather.8
  161.1 34.4 all-gather.10
  198.0 44.5 reduce-scatter.4
  245.0 44.5 reduce-scatter.6
  327.4 74.9 reduce-scatter.10
  405.5 31.6 reduce-scatter.8
  440.3 56.7 all-reduce.1
